TPU v7x, 32 devices: a whole 2x2x4 slice. The times are simulated.
32 devices in a mesh: groups: 2 (over y), seq: 16 (over z, x, core).
Axes of the slice: x: 2, y: 2, z: 4, core: 2. Of those that a mesh axis runs over, the one named last changes fastest.
Arguments:
- qkv: bfloat16 [4096, 32, 384], P(('groups', 'seq')), parts along dimension 0
- routes: int32 [4096, 32], P(('groups', 'seq')), parts along dimension 0, may hold values from 0 to 1, as said below
Outputs:
- attended: bfloat16 [4096, 32, 128], P(('groups', 'seq')), parts along dimension 0
There are 2 independent parts, one for each index of `groups`. A program takes and returns all parts, laid end to end along the dimension named above; each array names one. Nothing has to cross between parts.
Inputs may be any that keep to these rules, and one draw needn't show every extreme that they name: Every cluster of every head holds between 512 and 1536 tokens, and in every head some cluster holds exactly 1536. Numbering the pairs (head h, cluster c) as h * 2 + c, the tokens of one device name each aligned group of 4 pairs exactly 256 times. Integer counts, offsets and slot indices derived from routes may cross between devices packed several to a 32-bit word.
All inputs are finite; a program needn't handle non-finite values.
Results may differ from a plain program's by a relative error of at most 0.0047.
Values may be sent and summed in bfloat16 or wider, within the bound.
No kernel may reach another device: no remote copies, remote signals or barrier semaphores. Data moves between devices by JAX's collectives and lax.ppermute only.
A program may use at most 128 MiB of HBM per device.

v0:
```python
import math
import jax
import jax.numpy as jnp
from jax import lax
from jax.sharding import PartitionSpec as P

CLEN = 1024


def entering(part, axis, combine, identity):
    place = lax.axis_index(axis)
    gathered = lax.all_gather(part, axis)
    state = jnp.zeros_like(part) + jnp.asarray(identity, part.dtype)

    def one(turn, state):
        return combine(state, lax.dynamic_index_in_dim(gathered, turn, 0, False))

    return lax.fori_loop(0, place, one, state)


def attend(queries, keys, values, start, scale):
    block_rows = queries.shape[1]
    span = keys.shape[1]
    scores = jnp.einsum("pqd,pkd->pqk", queries, keys, preferred_element_type=jnp.float32) * scale
    rows = start + jnp.arange(block_rows, dtype=jnp.int32)[:, None]
    cols = jnp.arange(span, dtype=jnp.int32)[None, :]
    scores = jnp.where((cols <= rows)[None], scores, -1e30)
    peak = jnp.max(scores, axis=2, keepdims=True)
    expo = jnp.exp(scores - peak)
    weights = (expo / jnp.sum(expo, axis=2, keepdims=True)).astype(jnp.bfloat16)
    return jnp.einsum("pqk,pkd->pqd", weights, values, preferred_element_type=jnp.float32).astype(
        jnp.bfloat16
    )


def local(qkv, routes):
    tok, heads, width = qkv.shape
    head_size = width // 3
    nseq = lax.axis_size("seq")
    clusters = nseq * tok // CLEN
    pairs_dev = heads * tok // CLEN
    capacity = 3 * CLEN // 2
    block_rows = CLEN // 2
    share = CLEN // nseq
    rows_peer = pairs_dev * share
    total_pairs = heads * clusters
    scale = 1.0 / math.sqrt(head_size)
    member = routes[:, :, None] == jnp.arange(clusters, dtype=jnp.int32)[None, None, :]
    member_flat = member.reshape(tok, total_pairs)
    counts = jnp.sum(member_flat.astype(jnp.int32), axis=0)
    earlier = (jnp.arange(tok)[:, None] > jnp.arange(tok)[None, :]).astype(jnp.bfloat16)
    before = jnp.dot(earlier, member_flat.astype(jnp.bfloat16), preferred_element_type=jnp.float32)
    rank = jnp.sum(jnp.where(member, before.reshape(tok, heads, clusters), 0.0), axis=2).astype(
        jnp.int32
    )
    prefix = entering(counts, "seq", lambda first, second: first + second, jnp.zeros_like(counts))

    def lookup(table):
        return jnp.sum(jnp.where(member, table.reshape(heads, clusters)[None], 0), axis=2)

    group_counts = counts.reshape(total_pairs // pairs_dev, pairs_dev)
    within = (jnp.cumsum(group_counts, axis=1) - group_counts).reshape(total_pairs)
    slot = lookup(prefix) + rank
    pair_index = jnp.arange(heads, dtype=jnp.int32)[None, :] * clusters + routes
    owner = pair_index // pairs_dev
    local_pair = pair_index % pairs_dev
    position = (owner * rows_peer + lookup(within) + rank).reshape(tok * heads)
    target = (local_pair * capacity + slot).reshape(tok * heads)
    outgoing = (
        jnp.zeros((tok * heads, width), jnp.bfloat16)
        .at[position]
        .set(qkv.reshape(tok * heads, width))
    )
    labels = jnp.zeros((tok * heads,), jnp.int32).at[position].set(target)
    arrived, places = (
        lax.all_to_all(outgoing, "seq", split_axis=0, concat_axis=0, tiled=True),
        lax.all_to_all(labels, "seq", split_axis=0, concat_axis=0, tiled=True),
    )
    tiles = jnp.zeros((pairs_dev * capacity, width), jnp.bfloat16).at[places].set(arrived)
    tiles = tiles.reshape(pairs_dev, capacity, width)
    pieces = []
    for index in range(3):
        start = index * block_rows
        stop = start + block_rows
        pieces.append(
            attend(
                tiles[:, start:stop, :head_size],
                tiles[:, :stop, head_size : 2 * head_size],
                tiles[:, :stop, 2 * head_size :],
                start,
                scale,
            )
        )
    results = jnp.concatenate(pieces, axis=1)
    flat_results = results.reshape(pairs_dev * capacity, head_size)
    replies = flat_results[places]
    returned = lax.all_to_all(replies, "seq", split_axis=0, concat_axis=0, tiled=True)
    return returned[position].reshape(tok, heads, head_size)


def solution(mesh):
    placed = (P(("groups", "seq"), None, None), P(("groups", "seq"), None))
    return jax.shard_map(
        local,
        mesh=mesh,
        in_specs=placed,
        out_specs=P(("groups", "seq"), None, None),
        check_vma=False,
    )
```

profile of v0, /device:TPU:11, one launch (start us, length us, event | category | flops | bytes accessed | tf_op | source)
XLA Modules:
  0.0 283.6 jit_solution(1487217478119262765)
XLA Ops:
  0.0 0.8 convert_reduce_fusion
  0.8 0.1 copy.13
  0.9 0.1 reshape.224
  1.0 0.1 reshape.177
  1.1 15.5 %all-gather = s32[16,1,64]{2,1,0:T(1,128)S(1)} all-gather(s32[1,1,64]{2,1,0:T(1,128)S(1)} %reshape.224), channel_id=1, replica_groups=mesh['groups'=2,'seq'=16] {'seq'}, dimensions={0}, use_global_device_ids=true | all-gather | bytes 4352 | tf_op jit(solution)/shard_map/all_gather | solution.py:12
  16.6 0.2 while.10
  16.9 0.1 broadcast_in_dim.100
  17.0 0.1 copy.19
  17.0 0.2 reduce_window_sum.13
  17.2 0.1 reduce_window_sum.14
  17.3 0.1 copy.14
  17.4 0.1 eq.32
  17.5 0.7 eq.27.clone
  18.2 0.1 compare_bitcast_fusion
  18.3 0.9 fusion.30
  19.2 0.8 select_reduce_fusion
  20.0 0.8 fusion.47
  20.8 0.1 copy.17
  20.9 0.1 reshape.178
  21.1 0.1 copy.20
  21.1 0.1 reshape.204
  21.2 16.1 %scatter_custom_fusion = s32[4096]{0:T(1024)} fusion(s32[4096]{0:T(1024)S(1)} %bitcast.33, s32[4096]{0:T(1024)S(1)} %reshape.204, s32[]{:T(128)} %constant.29.clone.1), kind=kCustom, calls=%fused_computation.84 | custom fusion | bytes 16388 | tf_op jit(solution)/shard_map/scatter | solution.py:74
  37.3 9.8 %all-to-all-start = ((s32[16,256,1]{1,2,0:T(1,128)}), s32[16,256,1]{1,2,0:T(1,128)S(1)}, u32[]{:S(2)}, u32[]{:S(2)}) async-start(s32[16,256,1]{1,2,0:T(1,128)} %bitcast.6), calls=%async_computation | async-start | bytes 32768 | tf_op jit(solution)/shard_map/all_to_all | solution.py:77
  47.1 20.5 %scatter_custom_fusion.1 = bf16[4096,384]{1,0:T(8,128)(2,1)} fusion(s32[4096]{0:T(1024)S(1)} %bitcast.34, bf16[4096,384]{1,0:T(8,128)(2,1)} %bitcast.40, bf16[]{:T(256)} %constant.27.clone.1), kind=kCustom, calls=%fused_computation.41 | custom fusion | bytes 3146240 | tf_op jit(solution)/shard_map/scatter | solution.py:72
  67.7 0.0 all-to-all-done
  67.7 6.1 %all-to-all-start.1 = ((bf16[16,256,384]{2,1,0:T(8,128)(2,1)}), bf16[16,256,384]{2,1,0:T(8,128)(2,1)S(1)}, u32[]{:S(2)}, u32[]{:S(2)}) async-start(bf16[16,256,384]{2,1,0:T(8,128)(2,1)} %bitcast.10), calls=%async_computation.1 | async-start | bytes 6291456 | tf_op jit(solution)/shard_map/all_to_all | solution.py:76
  73.8 0.1 iota_compare_fusion.2
  73.8 1.2 iota_compare_fusion.1
  75.0 1.4 iota_compare_fusion
  76.4 67.2 %all-to-all-done.1 = bf16[16,256,384]{2,1,0:T(8,128)(2,1)S(1)} async-done(((bf16[16,256,384]{2,1,0:T(8,128)(2,1)}), bf16[16,256,384]{2,1,0:T(8,128)(2,1)S(1)}, u32[]{:S(2)}, u32[]{:S(2)}) %all-to-all-start.1) | async-done | bytes 3145760 | tf_op jit(solution)/shard_map/all_to_all | solution.py:76
  143.6 21.1 %scatter_custom_fusion.2 = bf16[6144,384]{1,0:T(8,128)(2,1)} fusion(s32[4096]{0:T(1024)S(1)} %bitcast.38, bf16[4096,384]{1,0:T(8,128)(2,1)S(1)} %bitcast.31, bf16[]{:T(256)} %constant.27.clone.1), kind=kCustom, calls=%fused_computation.30 | custom fusion | bytes 4718594 | tf_op jit(solution)/shard_map/scatter | solution.py:79
  164.8 8.1 %fusion.21 = f32[4,512,1536]{2,1,0:T(8,128)} fusion(bf16[4,1536,384]{2,1,0:T(8,128)(2,1)} %bitcast.25), kind=kOutput, calls=%fused_computation.38 | convolution fusion | flops 805306368 | bytes 14680064 | tf_op jit(solution)/shard_map/pqd,pkd->pqk/dot_general | solution.py:24
  172.8 0.0 copy-done
  172.8 4.5 %fusion.32 = f32[4,512,1024]{2,1,0:T(8,128)} fusion(bf16[4,1536,384]{2,1,0:T(8,128)(2,1)S(1)} %bitcast.26), kind=kOutput, calls=%fused_computation.49 | convolution fusion | flops 536870912 | bytes 9961472 | tf_op jit(solution)/shard_map/pqd,pkd->pqk/dot_general | solution.py:24
  177.3 2.8 fusion.37
  180.1 0.0 copy-done.2
  180.1 16.0 %fusion.58 = (f32[4,512]{1,0:T(4,128)S(1)}, f32[4,512,1536]{2,1,0:T(8,128)}) fusion(f32[4,512,1536]{2,1,0:T(8,128)} %fusion.21, pred[512,1536]{1,0:T(8,128)(4,1)S(1)} %copy-done.2), kind=kOutput, calls=%fused_computation.95 | output fusion | flops 18875904 | bytes 25960448 | tf_op jit(solution)/shard_map/sub | solution.py:29
  196.1 6.6 %fusion.27 = bf16[4,512,128]{2,1,0:T(8,128)(2,1)S(1)} fusion(bf16[4,1536,384]{2,1,0:T(8,128)(2,1)S(1)} %bitcast.28, f32[4,512,1536]{2,1,0:T(8,128)} %get-tuple-element.42, f32[4,512]{1,0:T(4,128)S(1)} %get-tuple-element.41), kind=kOutput, calls=%fused_computation.45 | convolution fusion | flops 811859968 | bytes 14688256 | tf_op jit(solution)/shard_map/pqk,pkd->pqd/dot_general | solution.py:31
  202.6 13.0 %fusion.59 = (f32[4,512]{1,0:T(4,128)S(1)}, f32[4,512,1024]{2,1,0:T(8,128)}) fusion(f32[4,512,1024]{2,1,0:T(8,128)} %fusion.32, pred[512,1024]{1,0:T(8,128)(4,1)S(1)} %copy-done.3), kind=kOutput, calls=%fused_computation.96 | output fusion | flops 12583935 | bytes 17309696 | tf_op jit(solution)/shard_map/sub | solution.py:29
  215.6 4.9 %fusion.25 = bf16[4,512,128]{2,1,0:T(8,128)(2,1)S(1)} fusion(f32[4,512,1024]{2,1,0:T(8,128)} %get-tuple-element.44, f32[4,512]{1,0:T(4,128)S(1)} %get-tuple-element.43, bf16[4,1536,384]{2,1,0:T(8,128)(2,1)S(1)} %bitcast.29), kind=kOutput, calls=%fused_computation.43 | convolution fusion | flops 541327360 | bytes 9969664 | tf_op jit(solution)/shard_map/pqk,pkd->pqd/dot_general | solution.py:31
  220.5 0.0 copy-done.1
  220.5 2.1 fusion.60
  222.7 1.0 fusion.26
  223.6 0.1 pad_maximum_fusion
  223.7 15.0 %gather_fusion = bf16[4096,128]{1,0:T(8,128)(2,1)} fusion(bf16[6144,128]{1,0:T(8,128)(2,1)S(1)} %bitcast.24, s32[4096]{0:T(1024)S(1)} %broadcast_clamp_fusion.1), kind=kCustom, calls=%fused_computation | custom fusion | bytes 2113536 | tf_op jit(solution)/shard_map/gather | solution.py:96
  238.8 4.9 %all-to-all-start.2 = ((bf16[16,256,128]{2,1,0:T(8,128)(2,1)}), bf16[16,256,128]{2,1,0:T(8,128)(2,1)S(1)}, u32[]{:S(2)}, u32[]{:S(2)}) async-start(bf16[16,256,128]{2,1,0:T(8,128)(2,1)} %bitcast.14), calls=%async_computation.2 | async-start | bytes 2097152 | tf_op jit(solution)/shard_map/all_to_all | solution.py:97
  243.7 24.9 %all-to-all-done.2 = bf16[16,256,128]{2,1,0:T(8,128)(2,1)S(1)} async-done(((bf16[16,256,128]{2,1,0:T(8,128)(2,1)}), bf16[16,256,128]{2,1,0:T(8,128)(2,1)S(1)}, u32[]{:S(2)}, u32[]{:S(2)}) %all-to-all-start.2) | async-done | bytes 1048608 | tf_op jit(solution)/shard_map/all_to_all | solution.py:97
  268.5 15.0 %gather_fusion.1 = bf16[4096,128]{1,0:T(8,128)(2,1)} fusion(bf16[4096,128]{1,0:T(8,128)(2,1)S(1)} %bitcast.23, s32[4096]{0:T(1024)S(1)} %broadcast_clamp_fusion), kind=kCustom, calls=%fused_computation.1 | custom fusion | bytes 2113536 | tf_op jit(solution)/shard_map/gather | solution.py:98
  (23 shorter events, 0.2 us)
Async XLA Ops:
  37.3 30.3 %all-to-all-start = ((s32[16,256,1]{1,2,0:T(1,128)}), s32[16,256,1]{1,2,0:T(1,128)S(1)}, u32[]{:S(2)}, u32[]{:S(2)}) async-start(s32[16,256,1]{1,2,0:T(1,128)} %bitcast.6), calls=%async_computation | async-start | bytes 32768 | tf_op jit(solution)/shard_map/all_to_all | solution.py:77
  67.7 76.0 %all-to-all-start.1 = ((bf16[16,256,384]{2,1,0:T(8,128)(2,1)}), bf16[16,256,384]{2,1,0:T(8,128)(2,1)S(1)}, u32[]{:S(2)}, u32[]{:S(2)}) async-start(bf16[16,256,384]{2,1,0:T(8,128)(2,1)} %bitcast.10), calls=%async_computation.1 | async-start | bytes 6291456 | tf_op jit(solution)/shard_map/all_to_all | solution.py:76
  164.7 8.1 %copy-start = (bf16[6144,384]{1,0:T(8,128)(2,1)S(1)}, bf16[6144,384]{1,0:T(8,128)(2,1)}, u32[]{:S(2)}) copy-start(bf16[6144,384]{1,0:T(8,128)(2,1)} %scatter_custom_fusion.2) | copy-start | bytes 14155780
  177.3 2.8 copy-start.2
  196.1 6.6 %copy-start.3 = (pred[512,1024]{1,0:T(8,128)(4,1)S(1)}, pred[512,1024]{1,0:T(8,128)(4,1)}, u32[]{:S(2)}) copy-start(pred[512,1024]{1,0:T(8,128)(4,1)} %iota_compare_fusion.1) | copy-start | bytes 1572868
  215.6 4.9 %copy-start.1 = (f32[4,512,512]{1,2,0:T(8,128)S(1)}, f32[4,512,512]{1,2,0:T(8,128)}, u32[]{:S(2)}) copy-start(f32[4,512,512]{1,2,0:T(8,128)} %fusion.37) | copy-start | bytes 12582916
  238.8 29.8 %all-to-all-start.2 = ((bf16[16,256,128]{2,1,0:T(8,128)(2,1)}), bf16[16,256,128]{2,1,0:T(8,128)(2,1)S(1)}, u32[]{:S(2)}, u32[]{:S(2)}) async-start(bf16[16,256,128]{2,1,0:T(8,128)(2,1)} %bitcast.14), calls=%async_computation.2 | async-start | bytes 2097152 | tf_op jit(solution)/shard_map/all_to_all | solution.py:97
where the time goes:
time: 284 us
  waiting for transfers between devices  92.1 us (32%)
  local copies, waits for them, and re-layouts  89.7 us (32%)
  other arithmetic  36.7 us (13%)
  matrix products  28.6 us (10%)
  starting transfers between devices  20.8 us (7%)
  blocking collectives  15.5 us (5%)
    all_to_all x1, waiting for transfers between devices, local(): lax.all_to_all(outgoing, 'seq', split_axis=0, concat_axis=0, tiled=True)  67.2 us
    sub x3, other arithmetic, attend(): expo = jnp.exp(scores - peak)  31.1 us
    all_to_all x1, waiting for transfers between devices, local(): lax.all_to_all(replies, 'seq', split_axis=0, concat_axis=0, tiled=True)  24.9 us
    scatter x1, local copies, waits for them, and re-layouts, local(): jnp.zeros((pairs_dev * capacity, width), jnp.bfloat16).at[places]  21.1 us
    scatter x1, local copies, waits for them, and re-layouts, local(): outgoing = jnp.zeros((tok * heads, width), jnp.bfloat16).at[position].set...  20.5 us
    scatter x1, local copies, waits for them, and re-layouts, local(): labels = jnp.zeros((tok * heads,), jnp.int32).at[position].set(target)  16.1 us
    all_gather x1, blocking collectives, entering(): gathered = lax.all_gather(part, axis)  15.5 us
    dot_general x3, matrix products, attend(): jnp.einsum('pqd,pkd->pqk', queries, keys, preferred_element_type=jnp.floa...  15.3 us
  transfers between devices with their start and end apart: 3, of which 2 were waited for; matrix products, arithmetic and copies ran while one was open for 8% of the time, Pallas kernels for 0%

commit v1 on v0

--- a/solution.py
+++ b/solution.py
@@ -5,6 +5,17 @@
 from jax.sharding import PartitionSpec as P
 
 CLEN = 1024
+
+
+def split_up(value, dim, length):
+    before, after = (value.shape[:dim], value.shape[dim + 1 :])
+    return jnp.moveaxis(value.reshape(*before, length, -1, *after), dim, 0)
+
+
+def in_order(blocks, dim):
+    lengths = list(blocks.shape[1:])
+    lengths[dim] *= blocks.shape[0]
+    return jnp.moveaxis(blocks, 0, dim).reshape(lengths)
 
 
 def entering(part, axis, combine, identity):
@@ -94,7 +105,15 @@
     results = jnp.concatenate(pieces, axis=1)
     flat_results = results.reshape(pairs_dev * capacity, head_size)
     replies = flat_results[places]
-    returned = lax.all_to_all(replies, "seq", split_axis=0, concat_axis=0, tiled=True)
+    length, index_2 = (lax.axis_size("seq"), lax.axis_index("seq"))
+    pieces_2 = split_up(replies, 0, length)
+    out = pieces_2
+    for lap in range(1, length):
+        target_2, source = ((index_2 + lap) % length, (index_2 - lap) % length)
+        sent = lax.dynamic_index_in_dim(pieces_2, target_2, 0)
+        received = lax.ppermute(sent, "seq", [(i, (i + lap) % length) for i in range(length)])
+        out = lax.dynamic_update_slice_in_dim(out, received, source, axis=0)
+    returned = in_order(out, 0)
     return returned[position].reshape(tok, heads, head_size)
 
 

time: 284 us -> 287 us (1.011)
  starting transfers between devices: 20.8 us -> 37.7 us
  waiting for transfers between devices: 92.1 us -> 79.8 us
    all_to_all x1 -> x0, waiting for transfers between devices: 24.9 us -> none  [local(): lax.all_to_all(replies, 'seq', split_axis=0, concat_axis=0, tiled=True)]
    ppermute x0 -> x15, starting transfers between devices: none -> 21.8 us  [local(): lax.ppermute(sent, 'seq', [(i, (i + lap) % length) for i in range(length)])]
    ppermute x0 -> x15, waiting for transfers between devices: none -> 10.8 us  [local(): lax.ppermute(sent, 'seq', [(i, (i + lap) % length) for i in range(length)])]
    all_to_all x1 -> x0, starting transfers between devices: 4.9 us -> none  [local(): lax.all_to_all(replies, 'seq', split_axis=0, concat_axis=0, tiled=True)]
    gather x1, local copies, waits for them, and re-layouts: 15 us -> 12.1 us  [local(): replies = flat_results[places]]
  transfers between devices with their start and end apart: 3 -> 17, of which waited for: 2 -> 8; matrix products, arithmetic and copies ran while one was open for 8% -> 8% of each run, Pallas kernels for 0% -> 0%
where the time goes in v1:
time: 287 us; the launch traced here: 285 us
  local copies, waits for them, and re-layouts  87.5 us (30%)
  waiting for transfers between devices  79.8 us (28%)
  starting transfers between devices  37.7 us (13%)
  other arithmetic  34.9 us (12%)
  matrix products  28.5 us (10%)
  blocking collectives  15.5 us (5%)
    all_to_all x1, waiting for transfers between devices, local(): lax.all_to_all(outgoing, 'seq', split_axis=0, concat_axis=0, tiled=True)  69 us
    sub x3, other arithmetic, attend(): expo = jnp.exp(scores - peak)  31 us
    ppermute x15, starting transfers between devices, local(): lax.ppermute(sent, 'seq', [(i, (i + lap) % length) for i in range(length)])  21.8 us
    scatter x1, local copies, waits for them, and re-layouts, local(): jnp.zeros((pairs_dev * capacity, width), jnp.bfloat16).at[places]  21.3 us
    scatter x1, local copies, waits for them, and re-layouts, local(): outgoing = jnp.zeros((tok * heads, width), jnp.bfloat16).at[position].set...  20.6 us
    scatter x1, local copies, waits for them, and re-layouts, local(): labels = jnp.zeros((tok * heads,), jnp.int32).at[position].set(target)  16.1 us
    all_gather x1, blocking collectives, entering(): gathered = lax.all_gather(part, axis)  15.5 us
    dot_general x3, matrix products, attend(): jnp.einsum('pqd,pkd->pqk', queries, keys, preferred_element_type=jnp.floa...  15.3 us
  transfers between devices with their start and end apart: 17, of which 8 were waited for; matrix products, arithmetic and copies ran while one was open for 8% of the time, Pallas kernels for 0%

profile of v1, /device:TPU:11, one launch (start us, length us, event | category | flops | bytes accessed | tf_op | source)
XLA Modules:
  0.0 284.6 jit_solution(5605388151883515149)
XLA Ops:
  0.0 0.8 convert_reduce_fusion
  0.9 0.1 reshape.230
  1.1 15.5 %all-gather = s32[16,1,64]{2,1,0:T(1,128)S(1)} all-gather(s32[1,1,64]{2,1,0:T(1,128)S(1)} %reshape.230), channel_id=1, replica_groups=mesh['groups'=2,'seq'=16] {'seq'}, dimensions={0}, use_global_device_ids=true | all-gather | bytes 4352 | tf_op jit(solution)/shard_map/all_gather | solution.py:23
  16.6 0.2 while.10
  17.0 0.2 reduce_window_sum.13
  17.4 0.1 eq.63
  17.5 0.7 eq.58.clone
  18.3 0.9 fusion.30
  19.2 0.8 select_reduce_fusion
  20.0 0.8 fusion.47
  20.8 0.1 copy.17
  20.9 0.1 reshape.182
  21.2 16.1 %scatter_custom_fusion = s32[4096]{0:T(1024)} fusion(s32[4096]{0:T(1024)S(1)} %bitcast.35, s32[4096]{0:T(1024)S(1)} %reshape.210, s32[]{:T(128)} %constant.242.clone.1), kind=kCustom, calls=%fused_computation.84 | custom fusion | bytes 16388 | tf_op jit(solution)/shard_map/scatter | solution.py:85
  37.3 9.8 %all-to-all-start = ((s32[16,256,1]{1,2,0:T(1,128)}), s32[16,256,1]{1,2,0:T(1,128)S(1)}, u32[]{:S(2)}, u32[]{:S(2)}) async-start(s32[16,256,1]{1,2,0:T(1,128)} %bitcast.6), calls=%async_computation | async-start | bytes 32768 | tf_op jit(solution)/shard_map/all_to_all | solution.py:88
  47.1 20.6 %scatter_custom_fusion.1 = bf16[4096,384]{1,0:T(8,128)(2,1)} fusion(s32[4096]{0:T(1024)S(1)} %bitcast.36, bf16[4096,384]{1,0:T(8,128)(2,1)} %bitcast.42, bf16[]{:T(256)} %constant.241.clone.1), kind=kCustom, calls=%fused_computation.41 | custom fusion | bytes 3146240 | tf_op jit(solution)/shard_map/scatter | solution.py:83
  67.7 6.1 %all-to-all-start.1 = ((bf16[16,256,384]{2,1,0:T(8,128)(2,1)}), bf16[16,256,384]{2,1,0:T(8,128)(2,1)}, u32[]{:S(2)}, u32[]{:S(2)}) async-start(bf16[16,256,384]{2,1,0:T(8,128)(2,1)} %bitcast.33), calls=%async_computation.1 | async-start | bytes 6291456 | tf_op jit(solution)/shard_map/all_to_all | solution.py:87
  73.9 0.4 iota_compare_fusion.1
  74.2 0.5 iota_compare_fusion
  74.8 69.0 %all-to-all-done.1 = bf16[16,256,384]{2,1,0:T(8,128)(2,1)} async-done(((bf16[16,256,384]{2,1,0:T(8,128)(2,1)}), bf16[16,256,384]{2,1,0:T(8,128)(2,1)}, u32[]{:S(2)}, u32[]{:S(2)}) %all-to-all-start.1) | async-done | bytes 3145760 | tf_op jit(solution)/shard_map/all_to_all | solution.py:87
  143.8 21.3 %scatter_custom_fusion.2 = bf16[6144,384]{1,0:T(8,128)(2,1)} fusion(s32[4096]{0:T(1024)S(1)} %bitcast.40, bf16[4096,384]{1,0:T(8,128)(2,1)} %bitcast.11, bf16[]{:T(256)} %constant.241.clone.1), kind=kCustom, calls=%fused_computation.30 | custom fusion | bytes 4719104 | tf_op jit(solution)/shard_map/scatter | solution.py:90
  165.1 8.1 %fusion.21 = f32[4,512,1536]{2,1,0:T(8,128)} fusion(bf16[4,1536,384]{2,1,0:T(8,128)(2,1)} %bitcast.27), kind=kOutput, calls=%fused_computation.38 | convolution fusion | flops 805306368 | bytes 14680064 | tf_op jit(solution)/shard_map/pqd,pkd->pqk/dot_general | solution.py:35
  173.2 4.5 %fusion.32 = f32[4,512,1024]{2,1,0:T(8,128)} fusion(bf16[4,1536,384]{2,1,0:T(8,128)(2,1)S(1)} %bitcast.28), kind=kOutput, calls=%fused_computation.49 | convolution fusion | flops 536870912 | bytes 9961472 | tf_op jit(solution)/shard_map/pqd,pkd->pqk/dot_general | solution.py:35
  177.7 2.8 fusion.37
  180.4 16.0 %fusion.58 = (f32[4,512]{1,0:T(4,128)S(1)}, f32[4,512,1536]{2,1,0:T(8,128)}) fusion(f32[4,512,1536]{2,1,0:T(8,128)} %fusion.21, pred[512,1536]{1,0:T(8,128)(4,1)S(1)} %iota_compare_fusion), kind=kOutput, calls=%fused_computation.125 | output fusion | flops 18875904 | bytes 25960448 | tf_op jit(solution)/shard_map/sub | solution.py:40
  196.4 6.5 %fusion.27 = bf16[4,512,128]{2,1,0:T(8,128)(2,1)S(1)} fusion(bf16[4,1536,384]{2,1,0:T(8,128)(2,1)S(1)} %bitcast.30, f32[4,512,1536]{2,1,0:T(8,128)} %get-tuple-element.57, f32[4,512]{1,0:T(4,128)S(1)} %get-tuple-element.56), kind=kOutput, calls=%fused_computation.45 | convolution fusion | flops 811859968 | bytes 14688256 | tf_op jit(solution)/shard_map/pqk,pkd->pqd/dot_general | solution.py:42
  202.9 12.9 %fusion.59 = (f32[4,512]{1,0:T(4,128)S(1)}, f32[4,512,1024]{2,1,0:T(8,128)}) fusion(f32[4,512,1024]{2,1,0:T(8,128)} %fusion.32, pred[512,1024]{1,0:T(8,128)(4,1)S(1)} %iota_compare_fusion.1), kind=kOutput, calls=%fused_computation.126 | output fusion | flops 12583935 | bytes 17309696 | tf_op jit(solution)/shard_map/sub | solution.py:40
  215.8 4.9 %fusion.25 = bf16[4,512,128]{2,1,0:T(8,128)(2,1)S(1)} fusion(f32[4,512,1024]{2,1,0:T(8,128)} %get-tuple-element.59, f32[4,512]{1,0:T(4,128)S(1)} %get-tuple-element.58, bf16[4,1536,384]{2,1,0:T(8,128)(2,1)S(1)} %bitcast.31), kind=kOutput, calls=%fused_computation.43 | convolution fusion | flops 541327360 | bytes 9969664 | tf_op jit(solution)/shard_map/pqk,pkd->pqd/dot_general | solution.py:42
  220.8 2.1 fusion.60
  222.9 1.0 fusion.26
  223.9 0.1 pad_maximum_fusion
  224.0 12.1 %gather_fusion = bf16[4096,128]{1,0:T(8,128)(2,1)S(1)} fusion(bf16[6144,128]{1,0:T(8,128)(2,1)S(1)} %bitcast.26, s32[4096]{0:T(1024)S(1)} %broadcast_clamp_fusion.1), kind=kCustom, calls=%fused_computation | custom fusion | bytes 2113536 | tf_op jit(solution)/shard_map/gather | solution.py:107
  236.1 1.9 collective-permute-start
  238.1 1.3 collective-permute-done
  239.4 0.2 constant_dynamic-slice_fusion
  240.0 0.7 collective-permute-start.2
  240.7 4.1 %collective-permute-start.3 = (bf16[1,256,128]{2,1,0:T(8,128)(2,1)S(1)}, bf16[1,256,128]{2,1,0:T(8,128)(2,1)S(1)}, u32[]{:S(2)}, u32[]{:S(2)}) collective-permute-start(bf16[1,256,128]{2,1,0:T(8,128)(2,1)S(1)} %get-tuple-element.50), channel_id=1, source_target_pairs={{0,4},{1,5},{2,6},{3,7},{4,8},{5,9},{6,10},{7,11},{8,12},{9,13},{1... | collective-permute-start | bytes 196616 | tf_op jit(solution)/shard_map/ppermute | solution.py:114
  244.8 0.1 collective-permute-start.4
  244.9 3.1 %collective-permute-start.5 = (bf16[1,256,128]{2,1,0:T(8,128)(2,1)S(1)}, bf16[1,256,128]{2,1,0:T(8,128)(2,1)S(1)}, u32[]{:S(2)}, u32[]{:S(2)}) collective-permute-start(bf16[1,256,128]{2,1,0:T(8,128)(2,1)S(1)} %get-tuple-element.48), channel_id=1, source_target_pairs={{0,6},{1,7},{2,8},{3,9},{4,10},{5,11},{6,12},{7,13},{8,14},{9,15},... | collective-permute-start | bytes 196616 | tf_op jit(solution)/shard_map/ppermute | solution.py:114
  248.0 1.8 collective-permute-start.7
  249.9 1.6 collective-permute-start.8
  251.5 3.5 %collective-permute-done.4 = bf16[1,256,128]{2,1,0:T(8,128)(2,1)S(1)} collective-permute-done((bf16[1,256,128]{2,1,0:T(8,128)(2,1)S(1)}, bf16[1,256,128]{2,1,0:T(8,128)(2,1)S(1)}, u32[]{:S(2)}, u32[]{:S(2)}) %collective-permute-start.4) | collective-permute-done | bytes 65568 | tf_op jit(solution)/shard_map/ppermute | solution.py:114
  255.0 1.4 collective-permute-done.5
  256.4 4.5 %collective-permute-start.10 = (bf16[1,256,128]{2,1,0:T(8,128)(2,1)S(1)}, bf16[1,256,128]{2,1,0:T(8,128)(2,1)S(1)}, u32[]{:S(2)}, u32[]{:S(2)}) collective-permute-start(bf16[1,256,128]{2,1,0:T(8,128)(2,1)S(1)} %get-tuple-element.43), channel_id=1, source_target_pairs={{0,11},{1,12},{2,13},{3,14},{4,15},{5,0},{6,1},{7,2},{8,3},{9,4},{... | collective-permute-start | bytes 196616 | tf_op jit(solution)/shard_map/ppermute | solution.py:114
  261.2 3.6 %collective-permute-start.13 = (bf16[1,256,128]{2,1,0:T(8,128)(2,1)S(1)}, bf16[1,256,128]{2,1,0:T(8,128)(2,1)S(1)}, u32[]{:S(2)}, u32[]{:S(2)}) collective-permute-start(bf16[1,256,128]{2,1,0:T(8,128)(2,1)S(1)} %get-tuple-element.40), channel_id=1, source_target_pairs={{0,14},{1,15},{2,0},{3,1},{4,2},{5,3},{6,4},{7,5},{8,6},{9,7},{10,... | collective-permute-start | bytes 196616 | tf_op jit(solution)/shard_map/ppermute | solution.py:114
  265.0 1.1 collective-permute-done.11
  266.2 2.7 collective-permute-done.13
  268.9 0.7 collective-permute-done.14
  269.6 15.0 %gather_fusion.1 = bf16[4096,128]{1,0:T(8,128)(2,1)} fusion(bf16[4096,128]{1,0:T(8,128)(2,1)S(1)} %bitcast.25, s32[4096]{0:T(1024)S(1)} %broadcast_clamp_fusion), kind=kCustom, calls=%fused_computation.1 | custom fusion | bytes 2113536 | tf_op jit(solution)/shard_map/gather | solution.py:117
  (63 shorter events, 1.6 us)
Async XLA Ops:
  37.3 30.4 %all-to-all-start = ((s32[16,256,1]{1,2,0:T(1,128)}), s32[16,256,1]{1,2,0:T(1,128)S(1)}, u32[]{:S(2)}, u32[]{:S(2)}) async-start(s32[16,256,1]{1,2,0:T(1,128)} %bitcast.6), calls=%async_computation | async-start | bytes 32768 | tf_op jit(solution)/shard_map/all_to_all | solution.py:88
  67.7 76.1 %all-to-all-start.1 = ((bf16[16,256,384]{2,1,0:T(8,128)(2,1)}), bf16[16,256,384]{2,1,0:T(8,128)(2,1)}, u32[]{:S(2)}, u32[]{:S(2)}) async-start(bf16[16,256,384]{2,1,0:T(8,128)(2,1)} %bitcast.33), calls=%async_computation.1 | async-start | bytes 6291456 | tf_op jit(solution)/shard_map/all_to_all | solution.py:87
  165.1 8.1 %copy-start = (bf16[6144,384]{1,0:T(8,128)(2,1)S(1)}, bf16[6144,384]{1,0:T(8,128)(2,1)}, u32[]{:S(2)}) copy-start(bf16[6144,384]{1,0:T(8,128)(2,1)} %scatter_custom_fusion.2) | copy-start | bytes 14155780
  215.8 4.9 %copy-start.1 = (f32[4,512,512]{1,2,0:T(8,128)S(1)}, f32[4,512,512]{1,2,0:T(8,128)}, u32[]{:S(2)}) copy-start(f32[4,512,512]{1,2,0:T(8,128)} %fusion.37) | copy-start | bytes 12582916
  236.1 3.3 %collective-permute-start = (bf16[1,256,128]{2,1,0:T(8,128)(2,1)S(1)}, bf16[1,256,128]{2,1,0:T(8,128)(2,1)S(1)}, u32[]{:S(2)}, u32[]{:S(2)}) collective-permute-start(bf16[1,256,128]{2,1,0:T(8,128)(2,1)S(1)} %constant_dynamic-slice_fusion.14), channel_id=1, source_target_pairs={{0,1},{1,2},{2,3},{3,4},{4,5},{5,6},{6,7},{7,8},{8,9},{9,10},{10,1... | collective-permute-start | bytes 196616 | tf_op jit(solution)/shard_map/ppermute | solution.py:114
  239.6 8.4 %collective-permute-start.1 = (bf16[1,256,128]{2,1,0:T(8,128)(2,1)S(1)}, bf16[1,256,128]{2,1,0:T(8,128)(2,1)S(1)}, u32[]{:S(2)}, u32[]{:S(2)}) collective-permute-start(bf16[1,256,128]{2,1,0:T(8,128)(2,1)S(1)} %get-tuple-element.52), channel_id=1, source_target_pairs={{0,2},{1,3},{2,4},{3,5},{4,6},{5,7},{6,8},{7,9},{8,10},{9,11},{10,... | collective-permute-start | bytes 196616 | tf_op jit(solution)/shard_map/ppermute | solution.py:114
  240.0 8.0 %collective-permute-start.2 = (bf16[1,256,128]{2,1,0:T(8,128)(2,1)S(1)}, bf16[1,256,128]{2,1,0:T(8,128)(2,1)S(1)}, u32[]{:S(2)}, u32[]{:S(2)}) collective-permute-start(bf16[1,256,128]{2,1,0:T(8,128)(2,1)S(1)} %get-tuple-element.51), channel_id=1, source_target_pairs={{0,3},{1,4},{2,5},{3,6},{4,7},{5,8},{6,9},{7,10},{8,11},{9,12},{10... | collective-permute-start | bytes 196616 | tf_op jit(solution)/shard_map/ppermute | solution.py:114
  240.7 9.2 %collective-permute-start.3 = (bf16[1,256,128]{2,1,0:T(8,128)(2,1)S(1)}, bf16[1,256,128]{2,1,0:T(8,128)(2,1)S(1)}, u32[]{:S(2)}, u32[]{:S(2)}) collective-permute-start(bf16[1,256,128]{2,1,0:T(8,128)(2,1)S(1)} %get-tuple-element.50), channel_id=1, source_target_pairs={{0,4},{1,5},{2,6},{3,7},{4,8},{5,9},{6,10},{7,11},{8,12},{9,13},{1... | collective-permute-start | bytes 196616 | tf_op jit(solution)/shard_map/ppermute | solution.py:114
  244.8 10.2 %collective-permute-start.4 = (bf16[1,256,128]{2,1,0:T(8,128)(2,1)S(1)}, bf16[1,256,128]{2,1,0:T(8,128)(2,1)S(1)}, u32[]{:S(2)}, u32[]{:S(2)}) collective-permute-start(bf16[1,256,128]{2,1,0:T(8,128)(2,1)S(1)} %get-tuple-element.49), channel_id=1, source_target_pairs={{0,5},{1,6},{2,7},{3,8},{4,9},{5,10},{6,11},{7,12},{8,13},{9,14},{... | collective-permute-start | bytes 196616 | tf_op jit(solution)/shard_map/ppermute | solution.py:114
  244.9 11.5 %collective-permute-start.5 = (bf16[1,256,128]{2,1,0:T(8,128)(2,1)S(1)}, bf16[1,256,128]{2,1,0:T(8,128)(2,1)S(1)}, u32[]{:S(2)}, u32[]{:S(2)}) collective-permute-start(bf16[1,256,128]{2,1,0:T(8,128)(2,1)S(1)} %get-tuple-element.48), channel_id=1, source_target_pairs={{0,6},{1,7},{2,8},{3,9},{4,10},{5,11},{6,12},{7,13},{8,14},{9,15},... | collective-permute-start | bytes 196616 | tf_op jit(solution)/shard_map/ppermute | solution.py:114
  248.0 13.0 %collective-permute-start.6 = (bf16[1,256,128]{2,1,0:T(8,128)(2,1)S(1)}, bf16[1,256,128]{2,1,0:T(8,128)(2,1)S(1)}, u32[]{:S(2)}, u32[]{:S(2)}) collective-permute-start(bf16[1,256,128]{2,1,0:T(8,128)(2,1)S(1)} %get-tuple-element.47), channel_id=1, source_target_pairs={{0,7},{1,8},{2,9},{3,10},{4,11},{5,12},{6,13},{7,14},{8,15},{9,0},... | collective-permute-start | bytes 196616 | tf_op jit(solution)/shard_map/ppermute | solution.py:114
  248.0 13.1 %collective-permute-start.7 = (bf16[1,256,128]{2,1,0:T(8,128)(2,1)S(1)}, bf16[1,256,128]{2,1,0:T(8,128)(2,1)S(1)}, u32[]{:S(2)}, u32[]{:S(2)}) collective-permute-start(bf16[1,256,128]{2,1,0:T(8,128)(2,1)S(1)} %get-tuple-element.46), channel_id=1, source_target_pairs={{0,8},{1,9},{2,10},{3,11},{4,12},{5,13},{6,14},{7,15},{8,0},{9,1},... | collective-permute-start | bytes 196616 | tf_op jit(solution)/shard_map/ppermute | solution.py:114
  249.9 11.3 %collective-permute-start.8 = (bf16[1,256,128]{2,1,0:T(8,128)(2,1)S(1)}, bf16[1,256,128]{2,1,0:T(8,128)(2,1)S(1)}, u32[]{:S(2)}, u32[]{:S(2)}) collective-permute-start(bf16[1,256,128]{2,1,0:T(8,128)(2,1)S(1)} %get-tuple-element.45), channel_id=1, source_target_pairs={{0,9},{1,10},{2,11},{3,12},{4,13},{5,14},{6,15},{7,0},{8,1},{9,2},... | collective-permute-start | bytes 196616 | tf_op jit(solution)/shard_map/ppermute | solution.py:114
  255.0 9.8 %collective-permute-start.9 = (bf16[1,256,128]{2,1,0:T(8,128)(2,1)S(1)}, bf16[1,256,128]{2,1,0:T(8,128)(2,1)S(1)}, u32[]{:S(2)}, u32[]{:S(2)}) collective-permute-start(bf16[1,256,128]{2,1,0:T(8,128)(2,1)S(1)} %get-tuple-element.44), channel_id=1, source_target_pairs={{0,10},{1,11},{2,12},{3,13},{4,14},{5,15},{6,0},{7,1},{8,2},{9,3},... | collective-permute-start | bytes 196616 | tf_op jit(solution)/shard_map/ppermute | solution.py:114
  256.4 8.5 %collective-permute-start.10 = (bf16[1,256,128]{2,1,0:T(8,128)(2,1)S(1)}, bf16[1,256,128]{2,1,0:T(8,128)(2,1)S(1)}, u32[]{:S(2)}, u32[]{:S(2)}) collective-permute-start(bf16[1,256,128]{2,1,0:T(8,128)(2,1)S(1)} %get-tuple-element.43), channel_id=1, source_target_pairs={{0,11},{1,12},{2,13},{3,14},{4,15},{5,0},{6,1},{7,2},{8,3},{9,4},{... | collective-permute-start | bytes 196616 | tf_op jit(solution)/shard_map/ppermute | solution.py:114
  261.0 5.1 %collective-permute-start.11 = (bf16[1,256,128]{2,1,0:T(8,128)(2,1)S(1)}, bf16[1,256,128]{2,1,0:T(8,128)(2,1)S(1)}, u32[]{:S(2)}, u32[]{:S(2)}) collective-permute-start(bf16[1,256,128]{2,1,0:T(8,128)(2,1)S(1)} %get-tuple-element.42), channel_id=1, source_target_pairs={{0,12},{1,13},{2,14},{3,15},{4,0},{5,1},{6,2},{7,3},{8,4},{9,5},{1... | collective-permute-start | bytes 196616 | tf_op jit(solution)/shard_map/ppermute | solution.py:114
  261.1 5.0 %collective-permute-start.12 = (bf16[1,256,128]{2,1,0:T(8,128)(2,1)S(1)}, bf16[1,256,128]{2,1,0:T(8,128)(2,1)S(1)}, u32[]{:S(2)}, u32[]{:S(2)}) collective-permute-start(bf16[1,256,128]{2,1,0:T(8,128)(2,1)S(1)} %get-tuple-element.41), channel_id=1, source_target_pairs={{0,13},{1,14},{2,15},{3,0},{4,1},{5,2},{6,3},{7,4},{8,5},{9,6},{10... | collective-permute-start | bytes 196616 | tf_op jit(solution)/shard_map/ppermute | solution.py:114
  261.2 7.7 %collective-permute-start.13 = (bf16[1,256,128]{2,1,0:T(8,128)(2,1)S(1)}, bf16[1,256,128]{2,1,0:T(8,128)(2,1)S(1)}, u32[]{:S(2)}, u32[]{:S(2)}) collective-permute-start(bf16[1,256,128]{2,1,0:T(8,128)(2,1)S(1)} %get-tuple-element.40), channel_id=1, source_target_pairs={{0,14},{1,15},{2,0},{3,1},{4,2},{5,3},{6,4},{7,5},{8,6},{9,7},{10,... | collective-permute-start | bytes 196616 | tf_op jit(solution)/shard_map/ppermute | solution.py:114
  264.9 4.7 %collective-permute-start.14 = (bf16[1,256,128]{2,1,0:T(8,128)(2,1)S(1)}, bf16[1,256,128]{2,1,0:T(8,128)(2,1)S(1)}, u32[]{:S(2)}, u32[]{:S(2)}) collective-permute-start(bf16[1,256,128]{2,1,0:T(8,128)(2,1)S(1)} %get-tuple-element.39), channel_id=1, source_target_pairs={{0,15},{1,0},{2,1},{3,2},{4,3},{5,4},{6,5},{7,6},{8,7},{9,8},{10,9... | collective-permute-start | bytes 196616 | tf_op jit(solution)/shard_map/ppermute | solution.py:114
